TPU v7x, 32 devices: a whole 2x2x4 slice. The times are simulated.
32 devices in a mesh: dp: 8 (over z, y), space: 4 (over x, core).
Axes of the slice: x: 2, y: 2, z: 4, core: 2. Of those that a mesh axis runs over, the one named last changes fastest.
Arguments:
- volume: bfloat16 [8, 4, 32, 32, 32], P('dp', None, 'space'), may hold values from -6 to 6
- cotangent: bfloat16 [8, 64, 512], P('dp', None, 'space'), may hold values from -6 to 6
- conv_one: bfloat16 [32, 4, 3, 3, 3], replicated, may hold values from -0.625 to 0.625
- conv_two: bfloat16 [64, 32, 3, 3, 3], replicated, may hold values from -0.21875 to 0.21875
Outputs:
- out_two: bfloat16 [8, 64, 512], P('dp', None, 'space')
- grad_pre: bfloat16 [8, 32, 4096], P('dp', None, 'space')
- update_one: float32 [3456], replicated
- update_two: float32 [55296], replicated
All inputs are finite; a program needn't handle non-finite values.
Results may differ from a plain program's by a relative error of at most 0.0057.
Values may be sent and summed in bfloat16 or wider, within the bound.
A program may use at most 64 MiB of HBM per device.

v0:
```python
import jax
import jax.numpy as jnp
from jax import lax
from jax.sharding import PartitionSpec as P

damp_input = 0.1
damp_grad = 0.03


def passed_along(value, axis, steps):
    count = lax.axis_size(axis)
    leading, last = (max(0, -steps), min(count, count - steps))
    return lax.ppermute(value, axis, [(source, source + steps) for source in range(leading, last)])


def tap_stack(padded, out_depth, out_rows, out_cols):
    pieces = []
    for depth_tap in range(3):
        for row_tap in range(3):
            for col_tap in range(3):
                pieces.append(
                    padded[
                        :,
                        depth_tap : depth_tap + 2 * out_depth : 2,
                        row_tap : row_tap + 2 * out_rows : 2,
                        col_tap : col_tap + 2 * out_cols : 2,
                    ]
                )
    stacked = jnp.stack(pieces, axis=1)
    return stacked.reshape(stacked.shape[0] * 27, -1)


def spread_taps(columns, channels, out_depth, out_rows, out_cols):
    pieces = columns.reshape(channels, 27, out_depth, out_rows, out_cols)
    canvas = jnp.zeros(
        (channels, 2 * out_depth + 1, 2 * out_rows + 1, 2 * out_cols + 1), jnp.float32
    )
    for depth_tap in range(3):
        for row_tap in range(3):
            for col_tap in range(3):
                tap_number = depth_tap * 9 + row_tap * 3 + col_tap
                canvas = canvas.at[
                    :,
                    depth_tap : depth_tap + 2 * out_depth : 2,
                    row_tap : row_tap + 2 * out_rows : 2,
                    col_tap : col_tap + 2 * out_cols : 2,
                ].add(pieces[:, tap_number])
    return canvas


def silu_slope(pre_act):
    sigmoid_val = jax.nn.sigmoid(pre_act)
    return sigmoid_val * (1.0 + pre_act * (1.0 - sigmoid_val))


def damped_solve(matrix, rhs_terms):
    lower_factor = jnp.linalg.cholesky(matrix)
    return jax.scipy.linalg.cho_solve((lower_factor, True), rhs_terms)


def precondition(gram_in, gram_out, grad_sum, total_rows):
    in_mat = gram_in / total_rows + damp_input * jnp.eye(gram_in.shape[0], dtype=jnp.float32)
    out_mat = gram_out / total_rows + damp_grad * jnp.eye(gram_out.shape[0], dtype=jnp.float32)
    mean_grad = grad_sum / total_rows
    half_solved = damped_solve(in_mat, mean_grad.T).T
    return (damped_solve(out_mat, half_solved), mean_grad)


def on_device(volume, cotangent, conv_one, conv_two):
    local_volume = volume[0]
    cot_flat = cotangent[0]
    depth_len, row_count, col_count = (
        local_volume.shape[1],
        local_volume.shape[2],
        local_volume.shape[3],
    )
    width_one = conv_one.shape[0]
    width_two = conv_two.shape[0]
    weight_one = conv_one.reshape(width_one, -1)
    weight_two = conv_two.reshape(width_two, -1)
    lower_plane = passed_along(local_volume[:, depth_len - 1], "space", 1)
    extended = jnp.concatenate([lower_plane[:, None], local_volume], axis=1)
    padded = jnp.pad(extended, ((0, 0), (0, 0), (1, 0), (1, 0)))
    first_cols = tap_stack(padded, depth_len // 2, row_count // 2, col_count // 2)
    pre_one = jnp.dot(weight_one, first_cols, preferred_element_type=jnp.float32)
    act_one = (
        jax.nn.silu(pre_one)
        .astype(jnp.bfloat16)
        .reshape(width_one, depth_len // 2, row_count // 2, col_count // 2)
    )
    lower_act = passed_along(act_one[:, depth_len // 2 - 1], "space", 1)
    extended_two = jnp.concatenate([lower_act[:, None], act_one], axis=1)
    padded_two = jnp.pad(extended_two, ((0, 0), (0, 0), (1, 0), (1, 0)))
    second_cols = tap_stack(padded_two, depth_len // 4, row_count // 4, col_count // 4)
    out_two = jnp.dot(weight_two, second_cols, preferred_element_type=jnp.float32).astype(
        jnp.bfloat16
    )
    back_cols = jnp.dot(weight_two.T, cot_flat, preferred_element_type=jnp.float32)
    canvas = spread_taps(back_cols, width_one, depth_len // 4, row_count // 4, col_count // 4)
    grad_act = canvas[:, 1:, 1:, 1:]
    upper_part = passed_along(canvas[:, 0, 1:, 1:].astype(jnp.bfloat16), "space", -1).astype(
        jnp.float32
    )
    grad_act = grad_act.at[:, -1].add(upper_part)
    grad_pre = (grad_act.reshape(width_one, -1) * silu_slope(pre_one)).astype(jnp.bfloat16)
    in_one = jnp.dot(first_cols, first_cols.T, preferred_element_type=jnp.float32)
    gram_one = jnp.dot(grad_pre, grad_pre.T, preferred_element_type=jnp.float32)
    grad_one = jnp.dot(grad_pre, first_cols.T, preferred_element_type=jnp.float32)
    in_two = jnp.dot(second_cols, second_cols.T, preferred_element_type=jnp.float32)
    gram_two = jnp.dot(cot_flat, cot_flat.T, preferred_element_type=jnp.float32)
    grad_two = jnp.dot(cot_flat, second_cols.T, preferred_element_type=jnp.float32)
    summed = lax.psum((in_two, in_one, gram_one, grad_one, gram_two, grad_two), ("dp", "space"))
    total_in_two, total_in_one, total_gram_one, total_grad_one, total_gram_two, total_grad_two = (
        summed
    )
    device_count = lax.axis_size("dp") * lax.axis_size("space")
    rows_one = first_cols.shape[1] * device_count
    rows_two = cot_flat.shape[1] * device_count
    step_one, mean_one = precondition(total_in_one, total_gram_one, total_grad_one, rows_one)
    step_two, mean_two = precondition(total_in_two, total_gram_two, total_grad_two, rows_two)
    quad_form = jnp.sum(step_one * mean_one) + jnp.sum(step_two * mean_two)
    factor = jnp.sqrt((step_one.size + step_two.size) / quad_form)
    update_one = (factor * step_one).reshape(-1)
    update_two = (factor * step_two).reshape(-1)
    return (out_two[None], grad_pre[None], update_one, update_two)


def solution(mesh):
    in_specs = (P("dp", None, "space", None, None), P("dp", None, "space"), P(), P())
    out_specs = (P("dp", None, "space"), P("dp", None, "space"), P(), P())
    return jax.shard_map(
        on_device, mesh=mesh, in_specs=in_specs, out_specs=out_specs, check_vma=False
    )
```

profile of v0, /device:TPU:0, one launch (start us, length us, event | category | flops | bytes accessed | tf_op | source)
XLA Modules:
  0.0 933.9 jit_solution(1185647925688393770)
XLA Ops:
  21.5 8.7 scatter_fusion.1
  38.9 8.7 scatter_fusion.3
  65.0 8.7 scatter_fusion.6
  73.7 8.7 scatter_fusion.7
  117.1 8.9 scatter_fusion.12
  221.7 9.1 scatter_fusion.24
  390.8 104.5 %all-reduce.10.cloned.1.call-done = (f32[108,108]{1,0:T(8,128)}, f32[32,108]{1,0:T(8,128)}, f32[32,32]{1,0:T(8,128)}, f32[64,64]{1,0:T(8,128)}) async-done(((f32[108,108]{1,0:T(8,128)}, f32[32,108]{1,0:T(8,128)}, f32[32,32]{1,0:T(8,128)}, f32[64,64]{1,0:T(8,128)}), (f32[108,108]{1,0:T(8,128)}, f32[32,108]{1,0:T(8,128)}, f32[32,32]{1,0:T(8,128)}, f32[64,64]{1,0:T(8,128)})) %all-reduce.10.cloned.1.call-update) | async-done | bytes 80976 | tf_op jit(solution)/shard_map/psum | solution.py:112
  497.0 9.9 %cholesky.246 = f32[108,108]{1,0:T(8,128)S(1)} custom-call(f32[108,108]{1,0:T(8,128)S(1)} %fusion.98), custom_call_target="Cholesky" | custom-call | tf_op jit(solution)/shard_map/jit(cholesky)/cholesky | solution.py:57
  542.7 97.4 %all-reduce.12.cloned.1.call-done = (f32[864,864]{1,0:T(8,128)}, f32[64,864]{1,0:T(8,128)}) async-done(((f32[864,864]{1,0:T(8,128)}, f32[64,864]{1,0:T(8,128)}), (f32[864,864]{1,0:T(8,128)}, f32[64,864]{1,0:T(8,128)})) %all-reduce.12.cloned.1.call-update) | async-done | bytes 3207184 | tf_op jit(solution)/shard_map/psum | solution.py:112
  652.4 11.7 %cholesky.269 = f32[128,128]{1,0:T(8,128)S(1)} custom-call(f32[128,128]{1,0:T(8,128)S(1)} %cholesky.607), custom_call_target="Cholesky" | custom-call | tf_op jit(solution)/shard_map/jit(cholesky)/cholesky | solution.py:57
  665.1 9.8 %custom-call.91 = f32[1,128,128]{1,2,0:T(8,128)S(1)} custom-call(f32[1,128,128]{2,1,0:T(8,128)S(1)} %get-tuple-element.85), custom_call_target="InvertDiagBlocksLowerTriangular" | custom-call | tf_op jit(solution)/shard_map/jit(cholesky)/cholesky | solution.py:57
  678.4 12.5 %cholesky.492 = f32[128,128]{1,0:T(8,128)S(1)} custom-call(f32[128,128]{1,0:T(8,128)} %cholesky.611), custom_call_target="Cholesky" | custom-call | tf_op jit(solution)/shard_map/jit(cholesky)/cholesky | solution.py:57
  691.6 11.0 %custom-call.92 = f32[1,128,128]{1,2,0:T(8,128)S(1)} custom-call(f32[1,128,128]{2,1,0:T(8,128)} %get-tuple-element.82), custom_call_target="InvertDiagBlocksLowerTriangular" | custom-call | tf_op jit(solution)/shard_map/jit(cholesky)/cholesky | solution.py:57
  704.7 11.7 %cholesky.513 = f32[128,128]{1,0:T(8,128)S(1)} custom-call(f32[128,128]{1,0:T(8,128)S(1)} %cholesky.616), custom_call_target="Cholesky" | custom-call | tf_op jit(solution)/shard_map/jit(cholesky)/cholesky | solution.py:57
  716.5 9.8 %custom-call.93 = f32[1,128,128]{1,2,0:T(8,128)S(1)} custom-call(f32[1,128,128]{2,1,0:T(8,128)S(1)} %get-tuple-element.79), custom_call_target="InvertDiagBlocksLowerTriangular" | custom-call | tf_op jit(solution)/shard_map/jit(cholesky)/cholesky | solution.py:57
  728.3 11.9 %cholesky.532 = f32[128,128]{1,0:T(8,128)S(1)} custom-call(f32[128,128]{1,0:T(8,128)S(1)} %cholesky.621), custom_call_target="Cholesky" | custom-call | tf_op jit(solution)/shard_map/jit(cholesky)/cholesky | solution.py:57
  740.2 9.8 %custom-call.94 = f32[1,128,128]{1,2,0:T(8,128)S(1)} custom-call(f32[1,128,128]{2,1,0:T(8,128)S(1)} %get-tuple-element.76), custom_call_target="InvertDiagBlocksLowerTriangular" | custom-call | tf_op jit(solution)/shard_map/jit(cholesky)/cholesky | solution.py:57
  752.0 11.7 %cholesky.551 = f32[128,128]{1,0:T(8,128)S(1)} custom-call(f32[128,128]{1,0:T(8,128)S(1)} %cholesky.626), custom_call_target="Cholesky" | custom-call | tf_op jit(solution)/shard_map/jit(cholesky)/cholesky | solution.py:57
  763.8 9.8 %custom-call.95 = f32[1,128,128]{1,2,0:T(8,128)S(1)} custom-call(f32[1,128,128]{2,1,0:T(8,128)S(1)} %get-tuple-element.73), custom_call_target="InvertDiagBlocksLowerTriangular" | custom-call | tf_op jit(solution)/shard_map/jit(cholesky)/cholesky | solution.py:57
  775.4 11.9 %cholesky.571 = f32[128,128]{1,0:T(8,128)S(1)} custom-call(f32[128,128]{1,0:T(8,128)S(1)} %cholesky.631), custom_call_target="Cholesky" | custom-call | tf_op jit(solution)/shard_map/jit(cholesky)/cholesky | solution.py:57
  787.4 9.8 %custom-call.96 = f32[1,128,128]{1,2,0:T(8,128)S(1)} custom-call(f32[1,128,128]{2,1,0:T(8,128)S(1)} %get-tuple-element.70), custom_call_target="InvertDiagBlocksLowerTriangular" | custom-call | tf_op jit(solution)/shard_map/jit(cholesky)/cholesky | solution.py:57
  798.6 8.8 cholesky.592
  818.4 18.1 %while.2 = (s32[]{:T(128)}, f32[864,864]{1,0:T(8,128)}, s32[6,2]{0,1:T(2,128)S(1)}, f32[6,128,128]{2,1,0:T(8,128)S(1)}, s32[]{:T(128)}) while((s32[]{:T(128)}, f32[864,864]{1,0:T(8,128)}, s32[6,2]{0,1:T(2,128)S(1)}, f32[6,128,128]{2,1,0:T(8,128)S(1)}, s32[]{:T(128)}) %tuple.123), condition=%wide.while_cond.1, body=%wide.while_body.1.sunk | while | flops 2 | bytes 131189 | solution.py:58
  838.4 69.8 %custom-call.97 = f32[7,128,128]{1,2,0:T(8,128)S(1)} custom-call(f32[7,128,128]{2,1,0:T(8,128)} %pad_maximum_fusion), custom_call_target="InvertDiagBlocksLowerTriangular" | custom-call | tf_op jit(solution)/shard_map/jit(_cho_solve)/triangular_solve | solution.py:58
  (374 shorter events, 437.0 us)
Async XLA Ops:
  7.2 488.1 %all-reduce.10.cloned.1.call-start = ((), (), s32[]{:S(2)}) async-start(), calls=%async_computation | async-start | bytes 245760 | tf_op jit(solution)/shard_map/psum | solution.py:112
  239.5 10.6 %copy-start.8 = (bf16[1,4,8,32,32]{4,3,2,1,0:T(8,128)(2,1)S(1)}, bf16[1,4,8,32,32]{4,3,2,1,0:T(8,128)(2,1)}, u32[]{:S(2)}) copy-start(bf16[1,4,8,32,32]{4,3,2,1,0:T(8,128)(2,1)} %param.6) | copy-start | bytes 196612
  239.5 13.7 %copy-start.10 = (bf16[1,64,128]{2,1,0:T(8,128)(2,1)S(1)}, bf16[1,64,128]{2,1,0:T(8,128)(2,1)}, u32[]{:S(2)}) copy-start(bf16[1,64,128]{2,1,0:T(8,128)(2,1)} %param.7) | copy-start | bytes 49156
  239.5 15.7 %copy-start.12 = (bf16[32,4,3,3,3]{0,1,4,3,2:T(4,128)(2,1)S(1)}, bf16[32,4,3,3,3]{0,1,4,3,2:T(4,128)(2,1)}, u32[]{:S(2)}) copy-start(bf16[32,4,3,3,3]{0,1,4,3,2:T(4,128)(2,1)} %param.8) | copy-start | bytes 20740
  248.8 112.8 %collective-permute-start.2 = (bf16[32,16,16]{0,2,1:T(8,128)(2,1)}, bf16[32,16,16]{0,2,1:T(8,128)(2,1)}, u32[]{:S(2)}, u32[]{:S(2)}) collective-permute-start(bf16[32,16,16]{0,2,1:T(8,128)(2,1)} %fusion.66), channel_id=1, source_target_pairs={{1,0},{2,1},{3,2},{5,4},{6,5},{7,6},{9,8},{10,9},{11,10},{13,12},{... | collective-permute-start | bytes 49160 | tf_op jit(solution)/shard_map/ppermute | solution.py:13
  250.2 5.1 collective-permute-start
  362.8 20.5 %copy-start.4 = (bf16[32,1024]{1,0:T(8,128)(2,1)}, bf16[32,1024]{1,0:T(8,128)(2,1)S(1)}, u32[]{:S(2)}) copy-start(bf16[32,1024]{1,0:T(8,128)(2,1)S(1)} %get-tuple-element.67) | copy-start | bytes 196612
  363.0 6.1 collective-permute-start.1
  369.0 271.0 %all-reduce.12.cloned.1.call-start = ((), (), s32[]{:S(2)}) async-start(), calls=%async_computation.1 | async-start | bytes 6651904 | tf_op jit(solution)/shard_map/psum | solution.py:112
  643.9 4.6 copy-start
  650.8 1.6 copy-start.3
  652.4 12.0 %copy-start.5 = (f32[64,864]{1,0:T(8,128)S(1)}, f32[64,864]{1,0:T(8,128)}, u32[]{:S(2)}) copy-start(f32[64,864]{1,0:T(8,128)} %get-tuple-element.37) | copy-start | bytes 663556
  816.4 0.9 copy-start.13
  816.4 1.9 copy-start.7
  816.5 20.1 %copy-start.9 = (f32[128,32]{1,0:T(8,128)S(1)}, f32[128,32]{1,0:T(8,128)}, u32[]{:S(2)}) copy-start(f32[128,32]{1,0:T(8,128)} %pad_convert_fusion) | copy-start | bytes 49156
  816.7 1.7 copy-start.1
  836.5 78.4 %copy-start.2 = (f32[864,864]{1,0:T(8,128)S(1)}, f32[864,864]{1,0:T(8,128)}, u32[]{:S(2)}) copy-start(f32[864,864]{1,0:T(8,128)} %get-tuple-element.214) | copy-start | bytes 8957956
  913.3 8.2 copy-start.11
  914.9 7.1 copy-start.6
Sparse Core Ops, SparseCore 0:
  369.2 126.0 all-reduce.9
  500.9 139.1 all-reduce.11
where the time goes:
time: 946 us; the launch traced here: 934 us
  other arithmetic  507 us (54%)
  waiting for transfers between devices  202 us (21%)
  local copies, waits for them, and re-layouts  157 us (17%)
  matrix products  37.8 us (4%)
  between operations  22.1 us (2%)
    scatter-add x27, other arithmetic, spread_taps(): canvas = canvas.at[:, depth_tap:depth_tap + 2 * out_depth:2, row_tap:row_...  235 us
    psum x2, waiting for transfers between devices, on_device(): lax.psum((in_two, in_one, gram_one, grad_one, gram_two, grad_two), ('dp',...  202 us
    another operation x36, other arithmetic, damped_solve(): lower_factor = jnp.linalg.cholesky(matrix)  166 us
    another operation x13, other arithmetic, damped_solve(): return jax.scipy.linalg.cho_solve((lower_factor, True), rhs_terms)  91.3 us
    slice x54, local copies, waits for them, and re-layouts, tap_stack(): padded[:, depth_tap:depth_tap + 2 * out_depth:2, row_tap:row_tap + 2 * ou...  90.9 us
    unnamed x95, local copies, waits for them, and re-layouts  27 us
  transfers between devices with their start and end apart: 5, of which 2 were waited for; matrix products, arithmetic and copies ran while one was open for 19% of the time, Pallas kernels for 0%

commit v1 on v0

--- a/solution.py
+++ b/solution.py
@@ -109,7 +109,9 @@
     in_two = jnp.dot(second_cols, second_cols.T, preferred_element_type=jnp.float32)
     gram_two = jnp.dot(cot_flat, cot_flat.T, preferred_element_type=jnp.float32)
     grad_two = jnp.dot(cot_flat, second_cols.T, preferred_element_type=jnp.float32)
-    summed = lax.psum((in_two, in_one, gram_one, grad_one, gram_two, grad_two), ("dp", "space"))
+    summed = lax.psum(
+        lax.psum((in_two, in_one, gram_one, grad_one, gram_two, grad_two), "dp"), "space"
+    )
     total_in_two, total_in_one, total_gram_one, total_grad_one, total_gram_two, total_grad_two = (
         summed
     )

time: 946 us -> 996 us (1.053)
  waiting for transfers between devices: 202 us -> 250 us
    psum x2 -> x4, waiting for transfers between devices: 202 us -> 250 us  [the longest x2 172 us: on_device(): lax.psum((in_two, in_one, gram_one, grad_one, gram_two, grad_two), 'dp')]
    unnamed x95 -> x97, local copies, waits for them, and re-layouts: 27 us -> 27.1 us
  transfers between devices with their start and end apart: 5 -> 7, of which waited for: 2 -> 4; matrix products, arithmetic and copies ran while one was open for 19% -> 18% of each run, Pallas kernels for 0% -> 0%
where the time goes in v1:
time: 996 us; the launch traced here: 985 us
  other arithmetic  510 us (51%)
  waiting for transfers between devices  250 us (25%)
  local copies, waits for them, and re-layouts  157 us (16%)
  matrix products  37.2 us (4%)
  between operations  21.5 us (2%)
    scatter-add x27, other arithmetic, spread_taps(): canvas = canvas.at[:, depth_tap:depth_tap + 2 * out_depth:2, row_tap:row_...  235 us
    psum x2, waiting for transfers between devices, on_device(): lax.psum((in_two, in_one, gram_one, grad_one, gram_two, grad_two), 'dp')  172 us
    another operation x36, other arithmetic, damped_solve(): lower_factor = jnp.linalg.cholesky(matrix)  171 us
    slice x54, local copies, waits for them, and re-layouts, tap_stack(): padded[:, depth_tap:depth_tap + 2 * out_depth:2, row_tap:row_tap + 2 * ou...  91 us
    another operation x13, other arithmetic, damped_solve(): return jax.scipy.linalg.cho_solve((lower_factor, True), rhs_terms)  90.6 us
    psum x2, waiting for transfers between devices, on_device(): lax.psum(lax.psum((in_two, in_one, gram_one, grad_one, gram_two, grad_two...  77.7 us
    unnamed x97, local copies, waits for them, and re-layouts  27.1 us
  transfers between devices with their start and end apart: 7, of which 4 were waited for; matrix products, arithmetic and copies ran while one was open for 18% of the time, Pallas kernels for 0%

profile of v1, /device:TPU:0, one launch (start us, length us, event | category | flops | bytes accessed | tf_op | source)
XLA Modules:
  0.0 984.6 jit_solution(5324492522883427069)
XLA Ops:
  12.8 8.7 scatter_fusion
  38.9 8.7 scatter_fusion.3
  117.1 9.2 scatter_fusion.12
  221.9 8.9 scatter_fusion.24
  387.8 52.9 %all-reduce.14.cloned.1.call-done = (f32[108,108]{1,0:T(8,128)}, f32[32,108]{1,0:T(8,128)}, f32[32,32]{1,0:T(8,128)}, f32[64,64]{1,0:T(8,128)}) async-done(((f32[108,108]{1,0:T(8,128)}, f32[32,108]{1,0:T(8,128)}, f32[32,32]{1,0:T(8,128)}, f32[64,64]{1,0:T(8,128)}), (f32[108,108]{1,0:T(8,128)}, f32[32,108]{1,0:T(8,128)}, f32[32,32]{1,0:T(8,128)}, f32[64,64]{1,0:T(8,128)})) %all-reduce.14.cloned.1.call-update) | async-done | bytes 80976 | tf_op jit(solution)/shard_map/psum | solution.py:113
  443.3 31.1 %all-reduce.18.cloned.1.call-done = (f32[108,108]{1,0:T(8,128)}, f32[32,108]{1,0:T(8,128)}, f32[32,32]{1,0:T(8,128)}, f32[64,64]{1,0:T(8,128)}) async-done(((f32[108,108]{1,0:T(8,128)}, f32[32,108]{1,0:T(8,128)}, f32[32,32]{1,0:T(8,128)}, f32[64,64]{1,0:T(8,128)}), (f32[108,108]{1,0:T(8,128)}, f32[32,108]{1,0:T(8,128)}, f32[32,32]{1,0:T(8,128)}, f32[64,64]{1,0:T(8,128)})) %all-reduce.18.cloned.1.call-update) | async-done | bytes 80976 | tf_op jit(solution)/shard_map/psum | solution.py:112
  476.2 9.9 %cholesky.246 = f32[108,108]{1,0:T(8,128)S(1)} custom-call(f32[108,108]{1,0:T(8,128)S(1)} %fusion.98), custom_call_target="Cholesky" | custom-call | tf_op jit(solution)/shard_map/jit(cholesky)/cholesky | solution.py:57
  493.3 118.9 %all-reduce.16.cloned.1.call-done = (f32[864,864]{1,0:T(8,128)}, f32[64,864]{1,0:T(8,128)}) async-done(((f32[864,864]{1,0:T(8,128)}, f32[64,864]{1,0:T(8,128)}), (f32[864,864]{1,0:T(8,128)}, f32[64,864]{1,0:T(8,128)})) %all-reduce.16.cloned.1.call-update) | async-done | bytes 3207184 | tf_op jit(solution)/shard_map/psum | solution.py:113
  638.6 46.6 %all-reduce.20.cloned.1.call-done = (f32[864,864]{1,0:T(8,128)}, f32[64,864]{1,0:T(8,128)}) async-done(((f32[864,864]{1,0:T(8,128)}, f32[64,864]{1,0:T(8,128)}), (f32[864,864]{1,0:T(8,128)}, f32[64,864]{1,0:T(8,128)})) %all-reduce.20.cloned.1.call-update) | async-done | bytes 3207184 | tf_op jit(solution)/shard_map/psum | solution.py:112
  697.8 11.7 %cholesky.269 = f32[128,128]{1,0:T(8,128)S(1)} custom-call(f32[128,128]{1,0:T(8,128)S(1)} %cholesky.607), custom_call_target="Cholesky" | custom-call | tf_op jit(solution)/shard_map/jit(cholesky)/cholesky | solution.py:57
  710.4 9.8 custom-call.91
  723.8 13.2 %cholesky.492 = f32[128,128]{1,0:T(8,128)} custom-call(f32[128,128]{1,0:T(8,128)} %cholesky.611), custom_call_target="Cholesky" | custom-call | tf_op jit(solution)/shard_map/jit(cholesky)/cholesky | solution.py:57
  738.5 11.4 %custom-call.92 = f32[1,128,128]{1,2,0:T(8,128)} custom-call(f32[1,128,128]{2,1,0:T(8,128)} %get-tuple-element.88), custom_call_target="InvertDiagBlocksLowerTriangular" | custom-call | tf_op jit(solution)/shard_map/jit(cholesky)/cholesky | solution.py:57
  753.4 12.5 %cholesky.513 = f32[128,128]{1,0:T(8,128)S(1)} custom-call(f32[128,128]{1,0:T(8,128)} %cholesky.616), custom_call_target="Cholesky" | custom-call | tf_op jit(solution)/shard_map/jit(cholesky)/cholesky | solution.py:57
  766.6 10.6 %custom-call.93 = f32[1,128,128]{1,2,0:T(8,128)S(1)} custom-call(f32[1,128,128]{2,1,0:T(8,128)} %get-tuple-element.85), custom_call_target="InvertDiagBlocksLowerTriangular" | custom-call | tf_op jit(solution)/shard_map/jit(cholesky)/cholesky | solution.py:57
  779.3 11.9 %cholesky.532 = f32[128,128]{1,0:T(8,128)S(1)} custom-call(f32[128,128]{1,0:T(8,128)S(1)} %cholesky.621), custom_call_target="Cholesky" | custom-call | tf_op jit(solution)/shard_map/jit(cholesky)/cholesky | solution.py:57
  791.3 9.8 custom-call.94
  803.1 11.7 %cholesky.551 = f32[128,128]{1,0:T(8,128)S(1)} custom-call(f32[128,128]{1,0:T(8,128)S(1)} %cholesky.626), custom_call_target="Cholesky" | custom-call | tf_op jit(solution)/shard_map/jit(cholesky)/cholesky | solution.py:57
  814.8 9.8 custom-call.95
  826.4 12.1 %cholesky.571 = f32[128,128]{1,0:T(8,128)S(1)} custom-call(f32[128,128]{1,0:T(8,128)S(1)} %cholesky.631), custom_call_target="Cholesky" | custom-call | tf_op jit(solution)/shard_map/jit(cholesky)/cholesky | solution.py:57
  838.6 9.8 custom-call.96
  849.8 8.8 cholesky.592
  869.5 18.3 %while.2 = (s32[]{:T(128)}, f32[864,864]{1,0:T(8,128)}, s32[6,2]{0,1:T(2,128)S(1)}, f32[6,128,128]{2,1,0:T(8,128)S(1)}, s32[]{:T(128)}) while((s32[]{:T(128)}, f32[864,864]{1,0:T(8,128)}, s32[6,2]{0,1:T(2,128)S(1)}, f32[6,128,128]{2,1,0:T(8,128)S(1)}, s32[]{:T(128)}) %tuple.129), condition=%wide.while_cond.1, body=%wide.while_body.1.sunk | while | flops 2 | bytes 131189 | solution.py:58
  889.7 69.7 %custom-call.97 = f32[7,128,128]{1,2,0:T(8,128)S(1)} custom-call(f32[7,128,128]{2,1,0:T(8,128)} %pad_maximum_fusion), custom_call_target="InvertDiagBlocksLowerTriangular" | custom-call | tf_op jit(solution)/shard_map/jit(_cho_solve)/triangular_solve | solution.py:58
  (382 shorter events, 455.1 us)
Async XLA Ops:
  7.2 433.5 %all-reduce.14.cloned.1.call-start = ((), (), s32[]{:S(2)}) async-start(), calls=%async_computation | async-start | bytes 245760 | tf_op jit(solution)/shard_map/psum | solution.py:113
  239.5 10.6 %copy-start.8 = (bf16[1,4,8,32,32]{4,3,2,1,0:T(8,128)(2,1)S(1)}, bf16[1,4,8,32,32]{4,3,2,1,0:T(8,128)(2,1)}, u32[]{:S(2)}) copy-start(bf16[1,4,8,32,32]{4,3,2,1,0:T(8,128)(2,1)} %param.6) | copy-start | bytes 196612
  239.6 13.7 %copy-start.9 = (bf16[1,64,128]{2,1,0:T(8,128)(2,1)S(1)}, bf16[1,64,128]{2,1,0:T(8,128)(2,1)}, u32[]{:S(2)}) copy-start(bf16[1,64,128]{2,1,0:T(8,128)(2,1)} %param.7) | copy-start | bytes 49156
  239.6 14.5 %copy-start.13 = (bf16[32,4,3,3,3]{0,1,4,3,2:T(4,128)(2,1)S(1)}, bf16[32,4,3,3,3]{0,1,4,3,2:T(4,128)(2,1)}, u32[]{:S(2)}) copy-start(bf16[32,4,3,3,3]{0,1,4,3,2:T(4,128)(2,1)} %param.8) | copy-start | bytes 20740
  248.9 111.6 %collective-permute-start.2 = (bf16[32,16,16]{0,2,1:T(8,128)(2,1)}, bf16[32,16,16]{0,2,1:T(8,128)(2,1)}, u32[]{:S(2)}, u32[]{:S(2)}) collective-permute-start(bf16[32,16,16]{0,2,1:T(8,128)(2,1)} %fusion.66), channel_id=1, source_target_pairs={{1,0},{2,1},{3,2},{5,4},{6,5},{7,6},{9,8},{10,9},{11,10},{13,12},{... | collective-permute-start | bytes 49160 | tf_op jit(solution)/shard_map/ppermute | solution.py:13
  250.2 3.9 collective-permute-start
  361.6 20.6 %copy-start.4 = (bf16[32,1024]{1,0:T(8,128)(2,1)}, bf16[32,1024]{1,0:T(8,128)(2,1)S(1)}, u32[]{:S(2)}) copy-start(bf16[32,1024]{1,0:T(8,128)(2,1)S(1)} %get-tuple-element.73) | copy-start | bytes 196612
  361.8 6.2 collective-permute-start.1
  368.0 106.4 %all-reduce.18.cloned.1.call-start = ((), (), s32[]{:S(2)}) async-start(), calls=%async_computation.2 | async-start | bytes 245760 | tf_op jit(solution)/shard_map/psum | solution.py:112
  440.7 171.5 %all-reduce.16.cloned.1.call-start = ((), (), s32[]{:S(2)}) async-start(), calls=%async_computation.1 | async-start | bytes 6651904 | tf_op jit(solution)/shard_map/psum | solution.py:113
  441.6 243.6 %all-reduce.20.cloned.1.call-start = ((), (), s32[]{:S(2)}) async-start(), calls=%async_computation.3 | async-start | bytes 6651904 | tf_op jit(solution)/shard_map/psum | solution.py:112
  474.4 149.4 %copy-start.10 = (f32[64,64]{1,0:T(8,128)S(1)}, f32[64,64]{1,0:T(8,128)}, u32[]{:S(2)}) copy-start(f32[64,64]{1,0:T(8,128)} %get-tuple-element.41) | copy-start | bytes 49156
  474.4 162.1 %copy-start.12 = (f32[32,108]{1,0:T(8,128)S(1)}, f32[32,108]{1,0:T(8,128)}, u32[]{:S(2)}) copy-start(f32[32,108]{1,0:T(8,128)} %get-tuple-element.39) | copy-start | bytes 41476
  689.0 4.8 copy-start
  696.1 1.6 copy-start.3
  697.8 12.0 %copy-start.5 = (f32[64,864]{1,0:T(8,128)S(1)}, f32[64,864]{1,0:T(8,128)}, u32[]{:S(2)}) copy-start(f32[64,864]{1,0:T(8,128)} %get-tuple-element.43) | copy-start | bytes 663556
  867.6 0.9 copy-start.14
  867.6 1.9 copy-start.7
  867.9 1.7 copy-start.1
  887.8 78.3 %copy-start.2 = (f32[864,864]{1,0:T(8,128)S(1)}, f32[864,864]{1,0:T(8,128)}, u32[]{:S(2)}) copy-start(f32[864,864]{1,0:T(8,128)} %get-tuple-element.232) | copy-start | bytes 8957956
  964.6 8.2 copy-start.11
  966.2 7.1 copy-start.6
Sparse Core Ops, SparseCore 0:
  368.1 72.5 all-reduce.13
  443.2 31.1 all-reduce.17
  478.1 134.1 all-reduce.15
  614.5 70.6 all-reduce.19
